TPU v7x, 32 devices: a whole 2x2x4 slice. The times are simulated.
32 devices in a mesh: expert: 8 (over z, x), tensor: 4 (over y, core).
Axes of the slice: x: 2, y: 2, z: 4, core: 2. Of those that a mesh axis runs over, the one named last changes fastest.
Arguments:
- tokens: bfloat16 [8192, 2048], P(('expert', 'tensor')), may hold values from -6 to 6
- cotangent: bfloat16 [8192, 2048], P(('expert', 'tensor')), may hold values from -6 to 6
- routes: int32 [8192, 8], P(('expert', 'tensor')), may hold values from 0 to 15, all different within a row; in each aligned block of 256 rows (0 to 255, 256 to 511, ...) at most 170 rows name the same one
- norm_in: float32 [2048], replicated, may hold values from 0.5 to 1.5
- query_w: bfloat16 [2048, 2048], P(None, 'tensor'), may hold values from -0.125 to 0.125
- key_w: bfloat16 [2048, 2048], P(None, 'tensor'), may hold values from -0.125 to 0.125
- value_w: bfloat16 [2048, 2048], P(None, 'tensor'), may hold values from -0.125 to 0.125
- out_w: bfloat16 [2048, 2048], P('tensor'), may hold values from -1 to 1
- query_gain: float32 [128], replicated, may hold values from 0.1 to 1.9
- key_gain: float32 [128], replicated, may hold values from 0.1 to 1.9
- norm_mid: float32 [2048], replicated, may hold values from 0.5 to 1.5
- router_w: float32 [2048, 16], replicated, may hold values from -0.0625 to 0.0625
- gate_w: bfloat16 [16, 2048, 1024], P('expert'), may hold values from -0.125 to 0.125
- up_w: bfloat16 [16, 2048, 1024], P('expert'), may hold values from -0.125 to 0.125
- down_w: bfloat16 [16, 1024, 2048], P('expert'), may hold values from -0.875 to 0.875
Outputs:
- output: bfloat16 [8192, 2048], P(('expert', 'tensor'))
- input_grad: float32 [8192, 2048], P(('expert', 'tensor'))
- norm_in_grad: float32 [2048], replicated
- query_w_grad: float32 [2048, 2048], P('expert', 'tensor')
- key_w_grad: float32 [2048, 2048], P('expert', 'tensor')
- value_w_grad: float32 [2048, 2048], P('expert', 'tensor')
- out_w_grad: float32 [2048, 2048], P('tensor', 'expert')
- query_gain_grad: float32 [128], replicated
- key_gain_grad: float32 [128], replicated
- norm_mid_grad: float32 [2048], replicated
- router_w_grad: float32 [2048, 16], replicated
- gate_w_grad: float32 [16, 2048, 1024], P('expert', None, 'tensor')
- up_w_grad: float32 [16, 2048, 1024], P('expert', None, 'tensor')
- down_w_grad: float32 [16, 1024, 2048], P('expert', 'tensor')
Inputs may be any that keep to these rules, and one draw needn't show every extreme that they name: `routes`: each row names 8 different experts. Among the 256 rows of one device (aligned blocks), no expert is named by more than 170 rows, and in some block one expert is named by exactly 170.
All inputs are finite; a program needn't handle non-finite values.
Results may differ from a plain program's by a relative error of at most 0.02.
Values may be sent and summed in bfloat16 or wider, within the bound.
A program may use at most 320 MiB of HBM per device.

v0:
```python
import math
import jax
import jax.numpy as jnp
from jax import lax
from jax.sharding import PartitionSpec as P

epsilon = 1e-06
highest = lax.Precision.HIGHEST
contract_last = (((1,), (1,)), ((), ()))
contract_first = (((0,), (0,)), ((), ()))


def inverse_rms(values):
    return lax.rsqrt(jnp.mean(values * values, axis=-1, keepdims=True) + epsilon)


def norm_backward(grad_norm, values, inverse, norm_gain):
    weighted = grad_norm * norm_gain
    inner_mean = jnp.mean(weighted * values, axis=-1, keepdims=True)
    return inverse * weighted - values * inverse * inverse * inverse * inner_mean


def rotary_tables(length, head_width):
    half_dim = head_width // 2
    frequency = jnp.exp(
        -math.log(10000.0) * 2.0 * jnp.arange(half_dim, dtype=jnp.float32) / head_width
    )
    angles = jnp.arange(length, dtype=jnp.float32)[:, None] * frequency[None, :]
    return (jnp.cos(angles)[:, None, :], jnp.sin(angles)[:, None, :])


def rotate(values, cosine, sine_table):
    half_dim = values.shape[-1] // 2
    first_half = values[..., :half_dim]
    second_half = values[..., half_dim:]
    return jnp.concatenate(
        [
            first_half * cosine - second_half * sine_table,
            second_half * cosine + first_half * sine_table,
        ],
        axis=-1,
    )


def rotate_back(gradient, cosine, sine_table):
    half_dim = gradient.shape[-1] // 2
    first_half = gradient[..., :half_dim]
    second_half = gradient[..., half_dim:]
    return jnp.concatenate(
        [
            first_half * cosine + second_half * sine_table,
            second_half * cosine - first_half * sine_table,
        ],
        axis=-1,
    )


def swiglu_back(hidden_grad, gate_pre, up_pre):
    sigmoid_part = jax.nn.sigmoid(gate_pre)
    gate_back = (
        hidden_grad * up_pre * sigmoid_part * (1.0 + gate_pre * (1.0 - sigmoid_part))
    ).astype(jnp.bfloat16)
    up_back = (hidden_grad * gate_pre * sigmoid_part).astype(jnp.bfloat16)
    return (gate_back, up_back)


def per_device(
    tokens,
    cotangent,
    routes,
    norm_in,
    query_w,
    key_w,
    value_w,
    out_w,
    query_gain,
    key_gain,
    norm_mid,
    router_w,
    gate_w,
    up_w,
    down_w,
):
    rows_own = tokens.shape[0]
    model_width = tokens.shape[1]
    tensor_count = lax.axis_size("tensor")
    expert_count = lax.axis_size("expert")
    head_width = query_gain.shape[0]
    local_heads = query_w.shape[1] // head_width
    experts_local = gate_w.shape[0]
    experts_all = router_w.shape[1]
    top_count = routes.shape[1]
    hidden_width = gate_w.shape[2]
    factor = 1.0 / math.sqrt(head_width)
    cot_all = lax.all_gather(cotangent, "expert", axis=0, tiled=True)
    source = tokens.astype(jnp.float32)
    scale_in = inverse_rms(source)
    normed_low = (source * scale_in * norm_in).astype(jnp.bfloat16)
    gathered = lax.all_gather(normed_low, "tensor", axis=0, tiled=True)
    seq_len = gathered.shape[0]
    query_pre = jnp.dot(gathered, query_w, preferred_element_type=jnp.float32)
    key_pre = jnp.dot(gathered, key_w, preferred_element_type=jnp.float32)
    value_low = jnp.dot(gathered, value_w, preferred_element_type=jnp.float32).astype(jnp.bfloat16)
    cosine, sine_table = rotary_tables(seq_len, head_width)
    query_heads = query_pre.reshape(seq_len, local_heads, head_width)
    key_heads = key_pre.reshape(seq_len, local_heads, head_width)
    query_scale = inverse_rms(query_heads)
    key_scale = inverse_rms(key_heads)
    query_low = rotate(query_heads * query_scale * query_gain, cosine, sine_table).astype(
        jnp.bfloat16
    )
    key_low = rotate(key_heads * key_scale * key_gain, cosine, sine_table).astype(jnp.bfloat16)
    value_heads = value_low.reshape(seq_len, local_heads, head_width)
    block_rows = min(512, seq_len)
    block_count = seq_len // block_rows
    query_blocks = query_low.reshape(block_count, block_rows, local_heads, head_width)

    def attend(query_block):
        scores = (
            jnp.einsum("qhd,khd->hqk", query_block, key_low, preferred_element_type=jnp.float32)
            * factor
        )
        row_max = jnp.max(scores, axis=-1, keepdims=True)
        shifted = jnp.exp(scores - row_max)
        row_sum = jnp.sum(shifted, axis=-1, keepdims=True)
        probs_low = (shifted / row_sum).astype(jnp.bfloat16)
        mixture = jnp.einsum(
            "hqk,khd->qhd", probs_low, value_heads, preferred_element_type=jnp.float32
        )
        return (mixture.astype(jnp.bfloat16), (row_max + jnp.log(row_sum))[..., 0])

    attended_blocks, log_sums = lax.map(attend, query_blocks)
    attended = attended_blocks.reshape(seq_len, local_heads * head_width)
    attn_out = lax.psum_scatter(
        jnp.dot(attended, out_w, preferred_element_type=jnp.float32).astype(jnp.bfloat16),
        "tensor",
        scatter_dimension=0,
        tiled=True,
    ).astype(jnp.float32)
    middle = source + attn_out
    scale_mid = inverse_rms(middle)
    normed_mid = middle * scale_mid * norm_mid
    mid_low = normed_mid.astype(jnp.bfloat16)
    logits = jnp.dot(normed_mid, router_w, precision=highest, preferred_element_type=jnp.float32)
    route_mask = routes[:, :, None] == jnp.arange(experts_all, dtype=jnp.int32)[None, None, :]
    mask_float = route_mask.astype(jnp.float32)
    chosen = jnp.sum(mask_float * logits[:, None, :], axis=-1)
    gating = jax.nn.softmax(chosen, axis=-1)
    upstream = cotangent.astype(jnp.float32)
    gates = jnp.sum(mask_float * gating[:, :, None], axis=1)
    x_all = lax.all_gather(mid_low, "expert", axis=0, tiled=True)
    gates_all = lax.all_gather(gates, "expert", axis=0, tiled=True)
    first_expert = lax.axis_index("expert") * experts_local
    own_gates = lax.dynamic_slice_in_dim(gates_all, first_expert, experts_local, 1)
    part_width = hidden_width // tensor_count
    rows_all = x_all.shape[0]
    y_part = jnp.zeros((rows_all, model_width), jnp.float32)
    x_grad_part = jnp.zeros((rows_all, model_width), jnp.float32)
    gate_grads, gate_parts, up_parts, down_parts = ([], [], [], [])
    for e in range(experts_local):
        hidden_raw = lax.dot_general(
            cot_all, down_w[e], contract_last, preferred_element_type=jnp.float32
        )
        gate_pre = jnp.dot(x_all, gate_w[e], preferred_element_type=jnp.float32)
        up_pre = jnp.dot(x_all, up_w[e], preferred_element_type=jnp.float32)
        weight = own_gates[:, e : e + 1]
        hidden = gate_pre * jax.nn.sigmoid(gate_pre) * up_pre
        gate_grads.append(jnp.sum(hidden * hidden_raw, axis=1))
        hidden_low = (hidden * weight).astype(jnp.bfloat16)
        gate_back, up_back = swiglu_back(hidden_raw * weight, gate_pre, up_pre)
        y_part = y_part + jnp.dot(hidden_low, down_w[e], preferred_element_type=jnp.float32)
        x_grad_part = x_grad_part + lax.dot_general(
            gate_back, gate_w[e], contract_last, preferred_element_type=jnp.float32
        )
        x_grad_part = x_grad_part + lax.dot_general(
            up_back, up_w[e], contract_last, preferred_element_type=jnp.float32
        )
        gate_parts.append(
            jnp.einsum(
                "nd,ntf->tdf",
                x_all,
                gate_back.reshape(rows_all, tensor_count, part_width),
                preferred_element_type=jnp.float32,
            ).astype(jnp.bfloat16)
        )
        up_parts.append(
            jnp.einsum(
                "nd,ntf->tdf",
                x_all,
                up_back.reshape(rows_all, tensor_count, part_width),
                preferred_element_type=jnp.float32,
            ).astype(jnp.bfloat16)
        )
        down_parts.append(
            lax.dot_general(
                hidden_low, cot_all, contract_first, preferred_element_type=jnp.float32
            ).astype(jnp.bfloat16)
        )
    x_grad = lax.psum_scatter(
        x_grad_part.astype(jnp.bfloat16), "expert", scatter_dimension=0, tiled=True
    )
    expert_input_grad = x_grad.astype(jnp.float32)
    gate_grad_sent = jnp.stack(gate_grads, axis=-1)
    gate_grad_all = lax.all_to_all(
        gate_grad_sent, "expert", split_axis=0, concat_axis=0, tiled=True
    )
    gate_grad_dense = (
        gate_grad_all.reshape(expert_count, rows_own, experts_local)
        .transpose(1, 0, 2)
        .reshape(rows_own, experts_all)
    )
    gate_grad = jnp.sum(mask_float * gate_grad_dense[:, None, :], axis=-1)
    y_sum = lax.psum_scatter(y_part.astype(jnp.bfloat16), "expert", scatter_dimension=0, tiled=True)
    output = (middle + y_sum.astype(jnp.float32)).astype(jnp.bfloat16)

    def own_part(parts):
        return [
            lax.psum_scatter(p, "tensor", scatter_dimension=0, tiled=True).astype(jnp.float32)
            for p in parts
        ]

    gate_w_grad = jnp.concatenate(own_part(gate_parts), axis=0)
    up_w_grad = jnp.concatenate(own_part(up_parts), axis=0)
    down_w_grad = jnp.stack(own_part(down_parts), axis=0)
    inner_gate = jnp.sum(gating * gate_grad, axis=-1, keepdims=True)
    chosen_grad = gating * (gate_grad - inner_gate)
    logit_grad = jnp.sum(chosen_grad[:, :, None] * mask_float, axis=1)
    router_part = lax.dot_general(
        normed_mid,
        logit_grad,
        contract_first,
        precision=highest,
        preferred_element_type=jnp.float32,
    )
    normed_mid_grad = expert_input_grad + lax.dot_general(
        logit_grad, router_w, contract_last, precision=highest, preferred_element_type=jnp.float32
    )
    norm_mid_part = jnp.sum(normed_mid_grad * middle * scale_mid, axis=0)
    middle_grad = upstream + norm_backward(normed_mid_grad, middle, scale_mid, norm_mid)
    branch_low = middle_grad.astype(jnp.bfloat16)
    branch_all = lax.all_gather(branch_low, "tensor", axis=0, tiled=True)
    attended_grad = lax.dot_general(
        branch_all, out_w, contract_last, preferred_element_type=jnp.float32
    ).astype(jnp.bfloat16)
    out_w_part = lax.dot_general(
        attended, branch_all, contract_first, preferred_element_type=jnp.float32
    )
    grad_blocks = attended_grad.reshape(block_count, block_rows, local_heads, head_width)

    def attend_back(carry, inputs):
        key_total, value_total = carry
        query_block, grad_block, log_block = inputs
        scores = (
            jnp.einsum("qhd,khd->hqk", query_block, key_low, preferred_element_type=jnp.float32)
            * factor
        )
        probs = jnp.exp(scores - log_block[:, :, None])
        probs_low = probs.astype(jnp.bfloat16)
        value_total = value_total + jnp.einsum(
            "hqk,qhd->khd", probs_low, grad_block, preferred_element_type=jnp.float32
        )
        prob_grad = jnp.einsum(
            "qhd,khd->hqk", grad_block, value_heads, preferred_element_type=jnp.float32
        )
        delta = jnp.sum(probs * prob_grad, axis=-1, keepdims=True)
        score_low = (probs * (prob_grad - delta)).astype(jnp.bfloat16)
        query_part = (
            jnp.einsum("hqk,khd->qhd", score_low, key_low, preferred_element_type=jnp.float32)
            * factor
        )
        key_total = (
            key_total
            + jnp.einsum("hqk,qhd->khd", score_low, query_block, preferred_element_type=jnp.float32)
            * factor
        )
        return ((key_total, value_total), query_part)

    zero_heads = jnp.zeros((seq_len, local_heads, head_width), jnp.float32)
    (key_grad, value_total), query_parts = lax.scan(
        attend_back, (zero_heads, zero_heads), (query_blocks, grad_blocks, log_sums)
    )
    query_grad = query_parts.reshape(seq_len, local_heads, head_width)
    value_grad_low = value_total.reshape(seq_len, local_heads * head_width).astype(jnp.bfloat16)
    query_rot_grad = rotate_back(query_grad, cosine, sine_table)
    key_rot_grad = rotate_back(key_grad, cosine, sine_table)
    query_gain_part = jnp.sum(query_rot_grad * query_heads * query_scale, axis=(0, 1))
    key_gain_part = jnp.sum(key_rot_grad * key_heads * key_scale, axis=(0, 1))
    query_pre_grad = (
        norm_backward(query_rot_grad, query_heads, query_scale, query_gain)
        .reshape(seq_len, local_heads * head_width)
        .astype(jnp.bfloat16)
    )
    key_pre_grad = (
        norm_backward(key_rot_grad, key_heads, key_scale, key_gain)
        .reshape(seq_len, local_heads * head_width)
        .astype(jnp.bfloat16)
    )
    query_w_part = lax.dot_general(
        gathered, query_pre_grad, contract_first, preferred_element_type=jnp.float32
    )
    key_w_part = lax.dot_general(
        gathered, key_pre_grad, contract_first, preferred_element_type=jnp.float32
    )
    value_w_part = lax.dot_general(
        gathered, value_grad_low, contract_first, preferred_element_type=jnp.float32
    )
    summed = lax.dot_general(
        query_pre_grad, query_w, contract_last, preferred_element_type=jnp.float32
    )
    summed = summed + lax.dot_general(
        key_pre_grad, key_w, contract_last, preferred_element_type=jnp.float32
    )
    rows_grad = lax.psum_scatter(
        (
            summed
            + lax.dot_general(
                value_grad_low, value_w, contract_last, preferred_element_type=jnp.float32
            )
        ).astype(jnp.bfloat16),
        "tensor",
        scatter_dimension=0,
        tiled=True,
    ).astype(jnp.float32)
    norm_in_part = jnp.sum(rows_grad * source * scale_in, axis=0)
    input_grad = middle_grad + norm_backward(rows_grad, source, scale_in, norm_in)
    query_w_grad, key_w_grad, value_w_grad, out_w_grad = (
        lax.psum_scatter(
            query_w_part.astype(jnp.bfloat16), "expert", scatter_dimension=0, tiled=True
        ).astype(jnp.float32),
        lax.psum_scatter(
            key_w_part.astype(jnp.bfloat16), "expert", scatter_dimension=0, tiled=True
        ).astype(jnp.float32),
        lax.psum_scatter(
            value_w_part.astype(jnp.bfloat16), "expert", scatter_dimension=0, tiled=True
        ).astype(jnp.float32),
        lax.psum_scatter(
            out_w_part.astype(jnp.bfloat16), "expert", scatter_dimension=1, tiled=True
        ).astype(jnp.float32),
    )
    norm_in_grad, query_gain_grad, key_gain_grad, norm_mid_grad, router_w_grad = lax.psum(
        (norm_in_part, query_gain_part, key_gain_part, norm_mid_part, router_part),
        ("expert", "tensor"),
    )
    return (
        output,
        input_grad,
        norm_in_grad,
        query_w_grad,
        key_w_grad,
        value_w_grad,
        out_w_grad,
        query_gain_grad,
        key_gain_grad,
        norm_mid_grad,
        router_w_grad,
        gate_w_grad,
        up_w_grad,
        down_w_grad,
    )


def solution(mesh):
    placed = (
        P(("expert", "tensor"), None),
        P(("expert", "tensor"), None),
        P(("expert", "tensor"), None),
        P(),
        P(None, "tensor"),
        P(None, "tensor"),
        P(None, "tensor"),
        P("tensor", None),
        P(),
        P(),
        P(),
        P(),
        P("expert", None, None),
        P("expert", None, None),
        P("expert", None, None),
    )
    return jax.shard_map(
        per_device,
        mesh=mesh,
        in_specs=placed,
        out_specs=(
            P(("expert", "tensor"), None),
            P(("expert", "tensor"), None),
            P(),
            P("expert", "tensor"),
            P("expert", "tensor"),
            P("expert", "tensor"),
            P("tensor", "expert"),
            P(),
            P(),
            P(),
            P(),
            P("expert", None, "tensor"),
            P("expert", None, "tensor"),
            P("expert", "tensor", None),
        ),
        check_vma=False,
    )
```

profile of v0, /device:TPU:0, one launch (start us, length us, event | category | flops | bytes accessed | tf_op | source)
XLA Modules:
  0.0 1698.5 jit_solution(10612123125915313644)
XLA Ops:
  14.0 35.3 %all-gather.5.cloned.1.call-done = bf16[1024,2048]{1,0:T(8,128)(2,1)} async-done(((bf16[256,2048]{1,0:T(8,128)(2,1)}), bf16[1024,2048]{1,0:T(8,128)(2,1)}) %all-gather.5.cloned.1.call-update) | async-done | bytes 4194320 | tf_op jit(solution)/shard_map/all_gather | solution.py:99
  49.3 6.2 convolution_convert_fusion.8
  57.9 5.9 multiply_reduce_fusion.10
  66.7 6.5 multiply_reduce_fusion.9
  76.2 3.5 multiply_multiply_fusion.2
  83.5 16.2 while.27
  99.7 6.6 convolution_convert_fusion.2
  106.5 44.6 %reduce-scatter.15.cloned.1.call-done = bf16[256,2048]{1,0:T(8,128)(2,1)} async-done(((bf16[1024,2048]{1,0:T(8,128)(2,1)}), bf16[256,2048]{1,0:T(8,128)(2,1)}) %reduce-scatter.15.cloned.1.call-update) | async-done | bytes 1048592 | tf_op jit(solution)/shard_map/reduce_scatter | solution.py:134
  156.0 124.5 %all-gather.7.cloned.1.call-done = bf16[2048,2048]{1,0:T(8,128)(2,1)} async-done(((bf16[256,2048]{1,0:T(8,128)(2,1)}), bf16[2048,2048]{1,0:T(8,128)(2,1)}) %all-gather.7.cloned.1.call-update) | async-done | bytes 8388624 | tf_op jit(solution)/shard_map/all_gather | solution.py:151
  280.4 14.9 fusion.51
  295.4 13.2 fusion.55
  308.6 97.2 %all-gather.9.cloned.1.call-done = bf16[2048,2048]{1,0:T(8,128)(2,1)} async-done(((bf16[256,2048]{1,0:T(8,128)(2,1)}), bf16[2048,2048]{1,0:T(8,128)(2,1)}) %all-gather.9.cloned.1.call-update) | async-done | bytes 8388624 | tf_op jit(solution)/shard_map/all_gather | solution.py:95
  405.8 20.0 %multiply_reduce_fusion.3 = (f32[2048]{0:T(1024)S(1)}, f32[2048,1024]{0,1:T(8,128)}) fusion(f32[2048,1024]{0,1:T(8,128)} %fusion.51, f32[2048,1024]{0,1:T(8,128)} %fusion.55, bf16[2048,2048]{1,0:T(8,128)(2,1)} %all-gather.9.cloned.1.call-done, bf16[2,1024,2048]{2,1,0:T(8,128)(2,1)} %param.33), kind=kOutput, calls=%fused_computation.50 | convolution fusion | flops 8604612608 | bytes 37756928 | tf_op jit(solution)/shard_map/dot_general | solution.py:161
  425.7 12.6 fusion.39
  438.4 17.6 %fusion.43 = f32[2048,1024]{0,1:T(8,128)} fusion(bf16[2048,2048]{1,0:T(8,128)(2,1)} %all-gather.7.cloned.1.call-done, bf16[2,2048,1024]{2,1,0:T(8,128)(2,1)} %param.31), kind=kOutput, calls=%fused_computation.79 | convolution fusion | flops 8589934592 | bytes 20971520 | tf_op jit(solution)/shard_map/dot_general | solution.py:164
  456.0 17.1 %multiply_reduce_fusion.2 = (f32[2048]{0:T(1024)S(1)}, f32[2048,1024]{0,1:T(8,128)}) fusion(f32[2048,1024]{0,1:T(8,128)S(1)} %fusion.39, f32[2048,1024]{0,1:T(8,128)} %fusion.43, bf16[2048,2048]{1,0:T(8,128)(2,1)} %all-gather.9.cloned.1.call-done, bf16[2,1024,2048]{2,1,0:T(8,128)(2,1)} %param.33), kind=kOutput, calls=%fused_computation.49 | convolution fusion | flops 8604612608 | bytes 37756928 | tf_op jit(solution)/shard_map/dot_general | solution.py:161
  473.7 3.3 all-to-all-start
  477.1 3.2 fusion.98
  480.3 3.2 all-to-all-done
  483.8 30.6 %all_gather.17 = f32[2048,16]{0,1:T(8,128)S(1)} all-gather(f32[256,16]{0,1:T(8,128)S(1)} %get-tuple-element.252), channel_id=1, replica_groups=mesh['expert'=8,'tensor'=4] {'expert'}, dimensions={0}, use_global_device_ids=true | all-gather | bytes 147456 | tf_op jit(solution)/shard_map/all_gather | solution.py:152
  514.4 12.5 multiply_convert_fusion.1
  526.9 15.7 fusion.41
  542.6 9.2 multiply_convert_fusion.3
  551.8 16.7 fusion.53
  568.5 14.1 fusion.49
  582.6 25.5 %add_convert_fusion = bf16[2048,2048]{1,0:T(8,128)(2,1)} fusion(f32[2048,2048]{1,0:T(8,128)} %fusion.41, f32[2048,2048]{1,0:T(8,128)} %fusion.53, f32[2048,2048]{1,0:T(8,128)} %fusion.49, bf16[2048,1024]{0,1:T(8,128)(2,1)} %get-tuple-element.299, bf16[2,2048,1024]{2,1,0:T(8,128)(2,1)} %param.32), kind=kOutput, calls=%fused_computation.38 | convolution fusion | flops 8606711808 | bytes 67108864 | tf_op jit(solution)/shard_map/dot_general | solution.py:175
  608.2 147.1 %reduce-scatter.19.cloned.1.call-done = bf16[256,2048]{1,0:T(8,128)(2,1)} async-done(((bf16[2048,2048]{1,0:T(8,128)(2,1)}), bf16[256,2048]{1,0:T(8,128)(2,1)}) %reduce-scatter.19.cloned.1.call-update) | async-done | bytes 1048592 | tf_op jit(solution)/shard_map/reduce_scatter | solution.py:199
  755.4 4.9 multiply_reduce_fusion.4
  763.8 13.9 convert_bitcast_fusion.2
  777.8 14.1 convert_bitcast_fusion.3
  791.9 13.9 convert_bitcast_fusion
  805.8 15.0 convert_bitcast_fusion.1
  820.9 16.9 convolution_convert_fusion
  837.9 16.5 convolution_convert_fusion.1
  854.5 6.4 convolution_convert_fusion.7
  862.0 6.3 convolution_convert_fusion.3
  868.4 30.6 %while.28 = (s32[]{:T(128)}, f32[1024,4,128]{0,2,1:T(8,128)}, f32[1024,4,128]{0,2,1:T(8,128)}, f32[2,512,4,128]{3,1,0,2:T(8,128)}, bf16[2,512,4,128]{3,1,2,0:T(8...) while((s32[]{:T(128)}, f32[1024,4,128]{0,2,1:T(8,128)}, ...), condition=%wide.region_23.24_spmd.clone, body=%wide.region_21.23_spmd.clone.sunk | while | flops 2712401920 | bytes 137421200 | solution.py:279
  901.7 6.6 convolution_convert_fusion.4
  911.6 7.5 multiply_add_fusion
  924.5 3.2 fusion.92
  927.9 3.9 convolution_convert_fusion.6
  931.8 5.2 multiply_reduce_fusion.5
  940.0 3.2 fusion.96
  944.2 3.8 convolution_convert_fusion.5
  953.3 6.4 add_convert_fusion.2
  960.5 20.5 %fusion.47 = f32[2048,2048]{1,0:T(8,128)} fusion(bf16[2,1024,2048]{2,1,0:T(8,128)(2,1)} %param.33, f32[2048]{0:T(1024)S(1)} %bitcast.295, f32[2048,1024]{0,1:T(8,128)} %fusion.51, f32[2048,1024]{0,1:T(8,128)} %fusion.55), kind=kOutput, calls=%fused_computation.83 | convolution fusion | flops 8604614656 | bytes 37756928 | tf_op jit(solution)/shard_map/dot_general | solution.py:171
  980.9 21.9 %add_convert_fusion.1 = bf16[2048,2048]{1,0:T(8,128)(2,1)} fusion(f32[2048,2048]{1,0:T(8,128)} %fusion.47, bf16[2,1024,2048]{2,1,0:T(8,128)(2,1)} %param.33, f32[2048]{0:T(1024)S(1)} %bitcast.292, f32[2048,1024]{0,1:T(8,128)} %copy-done.15, f32[2048,1024]{0,1:T(8,128)} %fusion.43), kind=kOutput, calls=%fused_computation.39 | convolution fusion | flops 8613003264 | bytes 46145536 | tf_op jit(solution)/shard_map/dot_general | solution.py:171
  1004.1 3.4 fusion.97
  1007.6 4.3 maximum_convert_fusion
  1011.9 5.3 copy.112
  1017.2 3.8 maximum_convert_fusion.1
  1021.1 5.3 copy.113
  1026.4 7.7 reduce-scatter.41.cloned.1.call-done
  1034.2 47.1 %reduce-scatter.39.cloned.1.call-done = bf16[256,2048]{1,0:T(8,128)(2,1)} async-done(((bf16[1024,2048]{1,0:T(8,128)(2,1)}), bf16[256,2048]{1,0:T(8,128)(2,1)}) %reduce-scatter.39.cloned.1.call-update) | async-done | bytes 1048592 | tf_op jit(solution)/shard_map/reduce_scatter | solution.py:218
  1081.3 3.8 maximum_convert_fusion.2
  1085.1 68.0 %reduce-scatter.29.cloned.1.call-done = bf16[512,256]{1,0:T(8,128)(2,1)} async-done(((bf16[512,2048]{1,0:T(8,128)(2,1)}), bf16[512,256]{1,0:T(8,128)(2,1)}) %reduce-scatter.29.cloned.1.call-update) | async-done | bytes 262160 | tf_op jit(solution)/shard_map/reduce_scatter | solution.py:336
  1154.9 68.2 %reduce-scatter.27.cloned.1.call-done = bf16[256,512]{1,0:T(8,128)(2,1)} async-done(((bf16[2048,512]{1,0:T(8,128)(2,1)}), bf16[256,512]{1,0:T(8,128)(2,1)}) %reduce-scatter.27.cloned.1.call-update) | async-done | bytes 262160 | tf_op jit(solution)/shard_map/reduce_scatter | solution.py:333
  1224.8 68.2 %reduce-scatter.23.cloned.1.call-done = bf16[256,512]{1,0:T(8,128)(2,1)} async-done(((bf16[2048,512]{1,0:T(8,128)(2,1)}), bf16[256,512]{1,0:T(8,128)(2,1)}) %reduce-scatter.23.cloned.1.call-update) | async-done | bytes 262160 | tf_op jit(solution)/shard_map/reduce_scatter | solution.py:327
  1294.8 68.9 %reduce-scatter.25.cloned.1.call-done = bf16[256,512]{1,0:T(8,128)(2,1)} async-done(((bf16[2048,512]{1,0:T(8,128)(2,1)}), bf16[256,512]{1,0:T(8,128)(2,1)}) %reduce-scatter.25.cloned.1.call-update) | async-done | bytes 262160 | tf_op jit(solution)/shard_map/reduce_scatter | solution.py:330
  1365.5 44.1 %reduce-scatter.21.cloned.1.call-done = bf16[256,2048]{1,0:T(8,128)(2,1)} async-done(((bf16[1024,2048]{1,0:T(8,128)(2,1)}), bf16[256,2048]{1,0:T(8,128)(2,1)}) %reduce-scatter.21.cloned.1.call-update) | async-done | bytes 1048592 | tf_op jit(solution)/shard_map/reduce_scatter | solution.py:313
  1411.5 151.1 %reduce-scatter.17.cloned.1.call-done = bf16[256,2048]{1,0:T(8,128)(2,1)} async-done(((bf16[2048,2048]{1,0:T(8,128)(2,1)}), bf16[256,2048]{1,0:T(8,128)(2,1)}) %reduce-scatter.17.cloned.1.call-update) | async-done | bytes 1048592 | tf_op jit(solution)/shard_map/reduce_scatter | solution.py:213
  1562.6 6.3 fusion.84
  1568.9 39.5 %all-reduce = (f32[2048]{0:T(1024)}, f32[128]{0:T(128)}, f32[128]{0:T(128)}, f32[2048]{0:T(1024)}) all-reduce(f32[2048]{0:T(1024)S(1)} %get-tuple-element.249, f32[128]{0:T(128)S(1)} %bitcast_reduce_fusion.1, f32[128]{0:T(128)S(1)} %bitcast_reduce_fusion, ...), channel_id=1, replica_groups=mesh['expert'=8,'tensor'=4] {'expert','tensor'}, use_global_device_ids=true, to_apply=%region_29.30 | all-reduce | flops 4352 | bytes 34816 | tf_op jit(solution)/shard_map/psum | solution.py:340
  1608.5 81.7 %all-reduce.3.cloned.1.call-done = f32[2048,16]{0,1:T(8,128)} async-done(((f32[2048,16]{0,1:T(8,128)}), f32[2048,16]{0,1:T(8,128)}) %all-reduce.3.cloned.1.call-update) | async-done | bytes 131088 | tf_op jit(solution)/shard_map/psum | solution.py:340
  (277 shorter events, 109.0 us)
Async XLA Ops:
  7.2 50.8 %copy-start = (bf16[2048,512]{1,0:T(8,128)(2,1)S(1)}, bf16[2048,512]{1,0:T(8,128)(2,1)}, u32[]{:S(2)}) copy-start(bf16[2048,512]{1,0:T(8,128)(2,1)} %param.23) | copy-start | bytes 6291460
  7.2 42.1 %all-gather.5.cloned.1.call-start = ((), (), s32[]{:S(2)}) async-start(), calls=%async_computation.15 | async-start | bytes 5242880 | tf_op jit(solution)/shard_map/all_gather | solution.py:99
  12.0 139.1 %reduce-scatter.15.cloned.1.call-start = ((), (), s32[]{:S(2)}) async-start(), calls=%async_computation.16 | async-start | bytes 5242880 | tf_op jit(solution)/shard_map/reduce_scatter | solution.py:134
  14.0 65.8 %copy-start.19 = (f32[1024,64]{1,0:T(8,128)}, f32[1024,64]{1,0:T(8,128)S(1)}, u32[]{:S(2)}) copy-start(f32[1024,64]{1,0:T(8,128)S(1)} %get-tuple-element.323) | copy-start | bytes 786436
  14.0 65.8 %copy-start.21 = (f32[1024,64]{1,0:T(8,128)}, f32[1024,64]{1,0:T(8,128)S(1)}, u32[]{:S(2)}) copy-start(f32[1024,64]{1,0:T(8,128)S(1)} %get-tuple-element.324) | copy-start | bytes 786436
  63.8 12.4 copy-start.30
  73.3 2.9 copy-start.51
  73.3 2.9 copy-start.53
  73.3 6.5 copy-start.28
  99.7 6.7 copy-start.3
  99.7 6.7 copy-start.32
  106.4 46.4 %copy-start.35 = (f32[2048]{0:T(1024)S(1)}, f32[2048]{0:T(1024)}, u32[]{:S(2)}) copy-start(f32[2048]{0:T(1024)} %param.29) | copy-start | bytes 24580
  106.4 44.7 %copy-start.8 = (bf16[256,2048]{1,0:T(8,128)(2,1)S(1)}, bf16[256,2048]{1,0:T(8,128)(2,1)}, u32[]{:S(2)}) copy-start(bf16[256,2048]{1,0:T(8,128)(2,1)} %param.19) | copy-start | bytes 3145732
  106.4 174.0 %all-gather.7.cloned.1.call-start = ((), (), s32[]{:S(2)}) async-start(), calls=%async_computation.17 | async-start | bytes 9437184 | tf_op jit(solution)/shard_map/all_gather | solution.py:151
  152.8 607.5 %copy-start.44 = (f32[256]{0:T(256)}, f32[256]{0:T(256)S(1)}, u32[]{:S(2)}) copy-start(f32[256]{0:T(256)S(1)} %add_rsqrt_fusion.2) | copy-start | bytes 3076
  155.4 250.4 %all-gather.9.cloned.1.call-start = ((), (), s32[]{:S(2)}) async-start(), calls=%async_computation.19 | async-start | bytes 9437184 | tf_op jit(solution)/shard_map/all_gather | solution.py:95
  280.4 15.0 copy-start.55
  438.4 17.6 %copy-start.15 = (f32[2048,1024]{0,1:T(8,128)}, f32[2048,1024]{0,1:T(8,128)S(1)}, u32[]{:S(2)}) copy-start(f32[2048,1024]{0,1:T(8,128)S(1)} %fusion.39) | copy-start | bytes 25165828
  455.9 21.1 %copy-start.61 = (f32[2048,16]{0,1:T(8,128)S(1)}, f32[2048,16]{0,1:T(8,128)}, u32[]{:S(2)}) copy-start(f32[2048,16]{0,1:T(8,128)} %param.30) | copy-start | bytes 393220
  456.0 27.6 %copy-start.41 = (s32[256,8]{0,1:T(8,128)S(1)}, s32[256,8]{0,1:T(8,128)}, u32[]{:S(2)}) copy-start(s32[256,8]{0,1:T(8,128)} %param.21) | copy-start | bytes 24580
  473.7 9.9 all-to-all-start
  477.0 278.3 %reduce-scatter.19.cloned.1.call-start = ((), (), s32[]{:S(2)}) async-start(), calls=%async_computation.20 | async-start | bytes 9437184 | tf_op jit(solution)/shard_map/reduce_scatter | solution.py:199
  483.8 271.6 %copy-start.46 = (f32[256,16]{0,1:T(8,128)}, f32[256,16]{0,1:T(8,128)S(1)}, u32[]{:S(2)}) copy-start(f32[256,16]{0,1:T(8,128)S(1)} %get-tuple-element.251) | copy-start | bytes 49156
  514.4 306.5 %copy-start.37 = (f32[2048,1]{0,1:T(1,128)}, f32[2048,1]{0,1:T(1,128)S(1)}, u32[]{:S(2)}) copy-start(f32[2048,1]{0,1:T(1,128)S(1)} %get-tuple-element.321) | copy-start | bytes 24580
  514.4 323.4 %copy-start.39 = (f32[2048,1]{0,1:T(1,128)}, f32[2048,1]{0,1:T(1,128)S(1)}, u32[]{:S(2)}) copy-start(f32[2048,1]{0,1:T(1,128)S(1)} %get-tuple-element.322) | copy-start | bytes 24580
  526.9 15.7 copy-start.24
  526.9 15.7 slice-start
  526.9 15.7 slice-start.1
  551.8 16.7 copy-start.23
  608.2 246.3 %all-gather.11.cloned.1.call-start = ((), (), s32[]{:S(2)}) async-start(), calls=%async_computation.21 | async-start | bytes 5242880 | tf_op jit(solution)/shard_map/all_gather | solution.py:241
  755.4 6.3 copy-start.13
  755.4 6.3 copy-start.14
  760.3 17.4 %copy-start.48 = (f32[256]{0:T(256)}, f32[256]{0:T(256)S(1)}, u32[]{:S(2)}) copy-start(f32[256]{0:T(256)S(1)} %broadcast_multiply_fusion.3) | copy-start | bytes 3076
  763.8 243.8 %reduce-scatter.33.cloned.1.call-start = ((), (), s32[]{:S(2)}) async-start(), calls=%async_computation.29 | async-start | bytes 5242880 | tf_op jit(solution)/shard_map/reduce_scatter | solution.py:218
  777.7 229.9 %reduce-scatter.31.cloned.1.call-start = ((), (), s32[]{:S(2)}) async-start(), calls=%async_computation.28 | async-start | bytes 5242880 | tf_op jit(solution)/shard_map/reduce_scatter | solution.py:218
  791.8 225.4 %reduce-scatter.37.cloned.1.call-start = ((), (), s32[]{:S(2)}) async-start(), calls=%async_computation.31 | async-start | bytes 5242880 | tf_op jit(solution)/shard_map/reduce_scatter | solution.py:218
  805.8 211.5 %reduce-scatter.35.cloned.1.call-start = ((), (), s32[]{:S(2)}) async-start(), calls=%async_computation.30 | async-start | bytes 5242880 | tf_op jit(solution)/shard_map/reduce_scatter | solution.py:218
  820.9 213.3 %reduce-scatter.41.cloned.1.call-start = ((), (), s32[]{:S(2)}) async-start(), calls=%async_computation.33 | async-start | bytes 5242880 | tf_op jit(solution)/shard_map/reduce_scatter | solution.py:218
  837.8 243.4 %reduce-scatter.39.cloned.1.call-start = ((), (), s32[]{:S(2)}) async-start(), calls=%async_computation.32 | async-start | bytes 5242880 | tf_op jit(solution)/shard_map/reduce_scatter | solution.py:218
  854.4 298.7 %reduce-scatter.29.cloned.1.call-start = ((), (), s32[]{:S(2)}) async-start(), calls=%async_computation.26 | async-start | bytes 2359296 | tf_op jit(solution)/shard_map/reduce_scatter | solution.py:336
  862.0 6.4 copy-start.4
  862.0 6.4 copy-start.33
  868.3 354.7 %reduce-scatter.27.cloned.1.call-start = ((), (), s32[]{:S(2)}) async-start(), calls=%async_computation.25 | async-start | bytes 2359296 | tf_op jit(solution)/shard_map/reduce_scatter | solution.py:333
  874.8 2.7 copy-start.7
  889.9 2.7 copy-start.7
  901.7 6.7 copy-start.52
  908.3 3.2 copy-start.20
  908.3 3.2 copy-start.22
  908.3 384.7 %reduce-scatter.23.cloned.1.call-start = ((), (), s32[]{:S(2)}) async-start(), calls=%async_computation.23 | async-start | bytes 2359296 | tf_op jit(solution)/shard_map/reduce_scatter | solution.py:327
  911.6 7.5 copy-start.12
  921.5 3.0 copy-start.31
  924.4 3.4 copy-start.56
  927.9 3.9 copy-start.54
  931.8 431.9 %reduce-scatter.25.cloned.1.call-start = ((), (), s32[]{:S(2)}) async-start(), calls=%async_computation.24 | async-start | bytes 2359296 | tf_op jit(solution)/shard_map/reduce_scatter | solution.py:330
  937.1 2.9 copy-start.29
  940.0 4.2 copy-start.57
  948.0 461.6 %reduce-scatter.21.cloned.1.call-start = ((), (), s32[]{:S(2)}) async-start(), calls=%async_computation.22 | async-start | bytes 5242880 | tf_op jit(solution)/shard_map/reduce_scatter | solution.py:313
  959.8 21.2 %copy-start.38 = (f32[2048,1]{0,1:T(1,128)S(1)}, f32[2048,1]{0,1:T(1,128)}, u32[]{:S(2)}) copy-start(f32[2048,1]{0,1:T(1,128)} %copy-done.37) | copy-start | bytes 24580
  959.8 602.8 %reduce-scatter.17.cloned.1.call-start = ((), (), s32[]{:S(2)}) async-start(), calls=%async_computation.18 | async-start | bytes 9437184 | tf_op jit(solution)/shard_map/reduce_scatter | solution.py:213
  1002.9 687.3 %all-reduce.3.cloned.1.call-start = ((), (), s32[]{:S(2)}) async-start(), calls=%async_computation.27 | async-start | bytes 262144 | tf_op jit(solution)/shard_map/psum | solution.py:340
  1081.3 328.4 %copy-start.34 = (f32[2048]{0:T(1024)S(1)}, f32[2048]{0:T(1024)}, u32[]{:S(2)}) copy-start(f32[2048]{0:T(1024)} %param.22) | copy-start | bytes 24580
  1081.3 328.4 %copy-start.43 = (f32[256]{0:T(256)S(1)}, f32[256]{0:T(256)}, u32[]{:S(2)}) copy-start(f32[256]{0:T(256)} %copy-done.42) | copy-start | bytes 3076
  1085.1 477.5 %copy-start.49 = (f32[256]{0:T(256)S(1)}, f32[256]{0:T(256)}, u32[]{:S(2)}) copy-start(f32[256]{0:T(256)} %copy-done.48) | copy-start | bytes 3076
  1411.5 157.4 %copy-start.50 = (f32[2048]{0:T(1024)S(1)}, f32[2048]{0:T(1024)}, u32[]{:S(2)}) copy-start(f32[2048]{0:T(1024)} %get-tuple-element.247) | copy-start | bytes 24580
  (31 other events, 51.4 us)
Sparse Core Ops, SparseCore 0:
  12.1 37.1 all-gather.4
  106.5 44.5 reduce-scatter.14
  155.5 124.8 all-gather.6
  282.6 123.1 all-gather.8
  608.3 147.0 reduce-scatter.18
  763.9 33.4 all-gather.10
  799.9 44.5 reduce-scatter.32
  847.7 44.5 reduce-scatter.30
  895.4 44.5 reduce-scatter.36
  942.5 44.5 reduce-scatter.34
  989.6 44.5 reduce-scatter.40
  1036.7 44.5 reduce-scatter.38
  1084.8 68.2 reduce-scatter.28
  1156.5 66.5 reduce-scatter.26
  1226.4 66.5 reduce-scatter.22
  1297.0 66.6 reduce-scatter.24
  1366.1 43.4 reduce-scatter.20
  1413.5 149.0 reduce-scatter.16
  1568.7 121.4 all-reduce.2
where the time goes:
time: 1700 us
  waiting for transfers between devices  1060 us (62%)
  matrix products  404 us (24%)
  other arithmetic  99.1 us (6%)
  blocking collectives  70.1 us (4%)
  local copies, waits for them, and re-layouts  46.5 us (3%)
    reduce_scatter x1, waiting for transfers between devices, per_device(): lax.psum_scatter(y_part.astype(jnp.bfloat16), 'expert', scatter_dimension...  151 us
    reduce_scatter x1, waiting for transfers between devices, per_device(): lax.psum_scatter(x_grad_part.astype(jnp.bfloat16), 'expert', scatter_dime...  147 us
    all_gather x1, waiting for transfers between devices, per_device(): x_all = lax.all_gather(mid_low, 'expert', axis=0, tiled=True)  124 us
    all_gather x1, waiting for transfers between devices, per_device(): cot_all = lax.all_gather(cotangent, 'expert', axis=0, tiled=True)  97.2 us
    psum x1, waiting for transfers between devices, per_device(): lax.psum((norm_in_part, query_gain_part, key_gain_part, norm_mid_part, ro...  81.7 us
    reduce_scatter x1, waiting for transfers between devices, per_device(): lax.psum_scatter(key_w_part.astype(jnp.bfloat16), 'expert', scatter_dimen...  68.9 us
    reduce_scatter x1, waiting for transfers between devices, per_device(): lax.psum_scatter(query_w_part.astype(jnp.bfloat16), 'expert', scatter_dim...  68.2 us
    reduce_scatter x1, waiting for transfers between devices, per_device(): lax.psum_scatter(value_w_part.astype(jnp.bfloat16), 'expert', scatter_dim...  68.2 us
  transfers between devices with their start and end apart: 20, of which 15 were waited for; matrix products, arithmetic and copies ran while one was open for 18% of the time, Pallas kernels for 0%

commit v1 on v0

--- a/solution.py
+++ b/solution.py
@@ -8,6 +8,28 @@
 highest = lax.Precision.HIGHEST
 contract_last = (((1,), (1,)), ((), ()))
 contract_first = (((0,), (0,)), ((), ()))
+
+
+def in_order(blocks, dim):
+    blocks = jnp.moveaxis(blocks, 0, dim)
+    dims = blocks.shape
+    return blocks.reshape(*dims[:dim], dims[dim] * dims[dim + 1], *dims[dim + 2 :])
+
+
+def collect(x, axis, dim):
+    size = lax.axis_size(axis)
+    pairs = [(i, (i + 1) % size) for i in range(size)]
+    back = [(b, a) for a, b in pairs]
+    lower, upper = ([], [])
+    for hop in range(size - 1):
+        if hop % 2 == 0:
+            lower.append(lax.ppermute(lower[-1] if lower else x, axis, pairs))
+        else:
+            upper.append(lax.ppermute(upper[-1] if upper else x, axis, back))
+    tiles = jnp.stack([*lower[::-1], x, *upper])
+    shift = lax.axis_index(axis) - len(lower)
+    tiles = tiles[(jnp.arange(size) - shift) % size]
+    return in_order(tiles, dim)
 
 
 def inverse_rms(values):
@@ -148,7 +170,7 @@
     gating = jax.nn.softmax(chosen, axis=-1)
     upstream = cotangent.astype(jnp.float32)
     gates = jnp.sum(mask_float * gating[:, :, None], axis=1)
-    x_all = lax.all_gather(mid_low, "expert", axis=0, tiled=True)
+    x_all = collect(mid_low, "expert", 0)
     gates_all = lax.all_gather(gates, "expert", axis=0, tiled=True)
     first_expert = lax.axis_index("expert") * experts_local
     own_gates = lax.dynamic_slice_in_dim(gates_all, first_expert, experts_local, 1)

time: 1700 us -> 1610 us (0.947)
  waiting for transfers between devices: 1060 us -> 907 us
  starting transfers between devices: 4.91 us -> 35.2 us
  local copies, waits for them, and re-layouts: 46.5 us -> 72.2 us
    ppermute x0 -> x7, waiting for transfers between devices: none -> 155 us  [the longest x4 155 us: collect(): lower.append(lax.ppermute(lower[-1] if lower else x, axis, pairs))]
    all_gather x1 -> x0, waiting for transfers between devices: 124 us -> none  [per_device(): x_all = lax.all_gather(mid_low, 'expert', axis=0, tiled=True)]
    all_gather x1, waiting for transfers between devices: 97.2 us -> 0.01 us  [per_device(): cot_all = lax.all_gather(cotangent, 'expert', axis=0, tiled=True)]
    psum x1, waiting for transfers between devices: 81.7 us -> 0.01 us  [per_device(): lax.psum((norm_in_part, query_gain_part, key_gain_part, norm_mid_part, ro...]
    ppermute x0 -> x7, starting transfers between devices: none -> 30.1 us  [the longest x3 23.5 us: collect(): upper.append(lax.ppermute(upper[-1] if upper else x, axis, back))]
  transfers between devices with their start and end apart: 20 -> 26, of which waited for: 15 -> 16; matrix products, arithmetic and copies ran while one was open for 18% -> 22% of each run, Pallas kernels for 0% -> 0%
where the time goes in v1:
time: 1610 us; the launch traced here: 1600 us
  waiting for transfers between devices  907 us (56%)
  matrix products  404 us (25%)
  other arithmetic  99.1 us (6%)
  local copies, waits for them, and re-layouts  72.2 us (4%)
  blocking collectives  70 us (4%)
  starting transfers between devices  35.2 us (2%)
  between operations  16.4 us (1%)
    ppermute x4, waiting for transfers between devices, collect(): lower.append(lax.ppermute(lower[-1] if lower else x, axis, pairs))  155 us
    reduce_scatter x1, waiting for transfers between devices, per_device(): lax.psum_scatter(y_part.astype(jnp.bfloat16), 'expert', scatter_dimension...  151 us
    reduce_scatter x1, waiting for transfers between devices, per_device(): lax.psum_scatter(x_grad_part.astype(jnp.bfloat16), 'expert', scatter_dime...  144 us
    reduce_scatter x1, waiting for transfers between devices, per_device(): lax.psum_scatter(key_w_part.astype(jnp.bfloat16), 'expert', scatter_dimen...  69.1 us
    reduce_scatter x1, waiting for transfers between devices, per_device(): lax.psum_scatter(value_w_part.astype(jnp.bfloat16), 'expert', scatter_dim...  68.5 us
    reduce_scatter x1, waiting for transfers between devices, per_device(): lax.psum_scatter(query_w_part.astype(jnp.bfloat16), 'expert', scatter_dim...  68.4 us
    reduce_scatter x1, waiting for transfers between devices, per_device(): lax.psum_scatter(out_w_part.astype(jnp.bfloat16), 'expert', scatter_dimen...  67.8 us
    reduce_scatter x6, waiting for transfers between devices, own_part(): lax.psum_scatter(p, 'tensor', scatter_dimension=0, tiled=True)  54.9 us
  transfers between devices with their start and end apart: 26, of which 16 were waited for; matrix products, arithmetic and copies ran while one was open for 22% of the time, Pallas kernels for 0%

profile of v1, /device:TPU:0, one launch (start us, length us, event | category | flops | bytes accessed | tf_op | source)
XLA Modules:
  0.0 1604.5 jit_solution(2677052904935464488)
XLA Ops:
  14.9 35.3 %all-gather.4.cloned.1.call-done = bf16[1024,2048]{1,0:T(8,128)(2,1)} async-done(((bf16[256,2048]{1,0:T(8,128)(2,1)}), bf16[1024,2048]{1,0:T(8,128)(2,1)}) %all-gather.4.cloned.1.call-update) | async-done | bytes 4194320 | tf_op jit(solution)/shard_map/all_gather | solution.py:121
  50.1 6.2 convolution_convert_fusion.8
  58.8 5.9 multiply_reduce_fusion.10
  67.6 6.5 multiply_reduce_fusion.9
  77.1 3.5 multiply_multiply_fusion.2
  84.3 16.2 %while.27 = (s32[]{:T(128)}, bf16[2,512,4,128]{3,2,1,0:T(4,128)(2,1)}, f32[2,4,512]{2,1,0:T(4,128)S(1)}, bf16[2,512,4,128]{3,1,2,0:T(8,128)(2,1)}, bf16[1024,4,1...) while((s32[]{:T(128)}, bf16[2,512,4,128]{3,2,1,0:T(4,128)(2,1)}, ...), condition=%wide.region_6.7_spmd, body=%wide.region_3.6_spmd.sunk | while | flops 1092876288 | bytes 42008756 | solution.py:154
  100.5 6.6 convolution_convert_fusion.2
  107.3 44.6 %reduce-scatter.15.cloned.1.call-done = bf16[256,2048]{1,0:T(8,128)(2,1)} async-done(((bf16[1024,2048]{1,0:T(8,128)(2,1)}), bf16[256,2048]{1,0:T(8,128)(2,1)}) %reduce-scatter.15.cloned.1.call-update) | async-done | bytes 1048592 | tf_op jit(solution)/shard_map/reduce_scatter | solution.py:156
  157.7 26.3 %collective-permute-done = bf16[256,2048]{1,0:T(8,128)(2,1)S(1)} collective-permute-done((bf16[256,2048]{1,0:T(8,128)(2,1)}, bf16[256,2048]{1,0:T(8,128)(2,1)S(1)}, u32[]{:S(2)}, u32[]{:S(2)}) %collective-permute-start) | collective-permute-done | bytes 1048608 | tf_op jit(solution)/shard_map/ppermute | solution.py:26
  185.0 4.7 collective-permute-start.4
  189.7 39.6 %collective-permute-done.1 = bf16[256,2048]{1,0:T(8,128)(2,1)} collective-permute-done((bf16[256,2048]{1,0:T(8,128)(2,1)S(1)}, bf16[256,2048]{1,0:T(8,128)(2,1)}, u32[]{:S(2)}, u32[]{:S(2)}) %collective-permute-start.1) | collective-permute-done | bytes 1048608 | tf_op jit(solution)/shard_map/ppermute | solution.py:26
  231.9 14.8 collective-permute-start.5
  246.6 40.1 %collective-permute-done.2 = bf16[256,2048]{1,0:T(8,128)(2,1)} collective-permute-done((bf16[256,2048]{1,0:T(8,128)(2,1)}, bf16[256,2048]{1,0:T(8,128)(2,1)}, u32[]{:S(2)}, u32[]{:S(2)}) %collective-permute-start.2) | collective-permute-done | bytes 1048608 | tf_op jit(solution)/shard_map/ppermute | solution.py:26
  289.3 4.1 collective-permute-start.6
  293.3 49.3 %collective-permute-done.3 = bf16[256,2048]{1,0:T(8,128)(2,1)} collective-permute-done((bf16[256,2048]{1,0:T(8,128)(2,1)}, bf16[256,2048]{1,0:T(8,128)(2,1)}, u32[]{:S(2)}, u32[]{:S(2)}) %collective-permute-start.3) | collective-permute-done | bytes 1048608 | tf_op jit(solution)/shard_map/ppermute | solution.py:26
  358.7 8.5 gather_fusion
  367.2 14.8 fusion.31
  382.0 13.4 fusion.43
  395.4 13.6 fusion.35
  409.1 13.2 fusion.47
  422.3 19.7 %multiply_reduce_fusion.3 = (f32[2048]{0:T(1024)S(1)}, f32[2048,1024]{0,1:T(8,128)}) fusion(f32[2048,1024]{0,1:T(8,128)} %fusion.43, f32[2048,1024]{0,1:T(8,128)} %fusion.47, bf16[2048,2048]{1,0:T(8,128)(2,1)} %all-gather.6.cloned.1.call-done, bf16[2,1024,2048]{2,1,0:T(8,128)(2,1)} %param.33), kind=kOutput, calls=%fused_computation.43 | convolution fusion | flops 8604612608 | bytes 37756928 | tf_op jit(solution)/shard_map/dot_general | solution.py:183
  442.0 19.6 %multiply_reduce_fusion.2 = (f32[2048]{0:T(1024)S(1)}, f32[2048,1024]{0,1:T(8,128)}) fusion(f32[2048,1024]{0,1:T(8,128)} %fusion.31, f32[2048,1024]{0,1:T(8,128)} %fusion.35, bf16[2048,2048]{1,0:T(8,128)(2,1)} %all-gather.6.cloned.1.call-done, bf16[2,1024,2048]{2,1,0:T(8,128)(2,1)} %param.33), kind=kOutput, calls=%fused_computation.42 | convolution fusion | flops 8604612608 | bytes 37756928 | tf_op jit(solution)/shard_map/dot_general | solution.py:183
  462.2 3.6 all-to-all-start
  472.5 30.5 %all_gather.13 = f32[2048,16]{0,1:T(8,128)S(1)} all-gather(f32[256,16]{0,1:T(8,128)S(1)} %get-tuple-element.252), channel_id=1, replica_groups=mesh['expert'=8,'tensor'=4] {'expert'}, dimensions={0}, use_global_device_ids=true | all-gather | bytes 147456 | tf_op jit(solution)/shard_map/all_gather | solution.py:174
  503.1 12.5 multiply_convert_fusion.1
  515.6 15.8 fusion.33
  531.4 9.2 multiply_convert_fusion.3
  540.6 16.9 %fusion.45 = f32[2048,2048]{1,0:T(8,128)} fusion(bf16[2048,1024]{0,1:T(8,128)(2,1)} %get-tuple-element.302, bf16[2,2048,1024]{2,1,0:T(8,128)(2,1)} %param.31), kind=kOutput, calls=%fused_computation.82 | convolution fusion | flops 8589934592 | bytes 25165824 | tf_op jit(solution)/shard_map/dot_general | solution.py:194
  557.5 14.3 fusion.41
  571.7 25.4 %add_convert_fusion = bf16[2048,2048]{1,0:T(8,128)(2,1)} fusion(f32[2048,2048]{1,0:T(8,128)} %fusion.33, f32[2048,2048]{1,0:T(8,128)} %fusion.45, f32[2048,2048]{1,0:T(8,128)} %fusion.41, bf16[2048,1024]{0,1:T(8,128)(2,1)} %get-tuple-element.299, bf16[2,2048,1024]{2,1,0:T(8,128)(2,1)} %param.32), kind=kOutput, calls=%fused_computation.39 | convolution fusion | flops 8606711808 | bytes 67108864 | tf_op jit(solution)/shard_map/dot_general | solution.py:197
  597.2 144.3 %reduce-scatter.19.cloned.1.call-done = bf16[256,2048]{1,0:T(8,128)(2,1)} async-done(((bf16[2048,2048]{1,0:T(8,128)(2,1)}), bf16[256,2048]{1,0:T(8,128)(2,1)}) %reduce-scatter.19.cloned.1.call-update) | async-done | bytes 1048592 | tf_op jit(solution)/shard_map/reduce_scatter | solution.py:221
  741.5 4.9 multiply_reduce_fusion.4
  750.0 13.8 convert_bitcast_fusion.2
  763.9 14.1 convert_bitcast_fusion.3
  778.0 13.9 convert_bitcast_fusion
  791.9 15.0 convert_bitcast_fusion.1
  807.0 16.9 %convolution_convert_fusion = bf16[1024,2048]{1,0:T(8,128)(2,1)} fusion(bf16[2048,2048]{1,0:T(8,128)(2,1)} %all-gather.6.cloned.1.call-done, f32[2048]{0:T(1024)S(1)} %bitcast.307, f32[2048,1024]{0,1:T(8,128)} %fusion.31, f32[2048,1024]{0,1:T(8,128)} %fusion.35), kind=kOutput, calls=%fused_computation.95 | convolution fusion | flops 8606711808 | bytes 29368320 | tf_op jit(solution)/shard_map/dot_general | solution.py:217
  824.0 16.5 %convolution_convert_fusion.1 = bf16[1024,2048]{1,0:T(8,128)(2,1)} fusion(bf16[2048,2048]{1,0:T(8,128)(2,1)} %all-gather.6.cloned.1.call-done, f32[2048]{0:T(1024)S(1)} %bitcast.310, f32[2048,1024]{0,1:T(8,128)} %fusion.43, f32[2048,1024]{0,1:T(8,128)} %fusion.47), kind=kOutput, calls=%fused_computation.96 | convolution fusion | flops 8606711808 | bytes 29368320 | tf_op jit(solution)/shard_map/dot_general | solution.py:217
  840.6 6.3 convolution_convert_fusion.7
  848.1 6.3 convolution_convert_fusion.3
  854.5 30.6 %while.28 = (s32[]{:T(128)}, f32[1024,4,128]{0,2,1:T(8,128)}, f32[1024,4,128]{0,2,1:T(8,128)}, f32[2,512,4,128]{3,1,0,2:T(8,128)}, bf16[2,512,4,128]{3,1,2,0:T(8...) while((s32[]{:T(128)}, f32[1024,4,128]{0,2,1:T(8,128)}, ...), condition=%wide.region_23.24_spmd.clone, body=%wide.region_21.23_spmd.clone.sunk | while | flops 2712401920 | bytes 137421200 | solution.py:301
  887.9 7.0 convolution_convert_fusion.4
  898.1 7.4 multiply_add_fusion
  914.5 3.9 convolution_convert_fusion.6
  918.4 5.3 multiply_reduce_fusion.5
  930.9 3.8 convolution_convert_fusion.5
  940.1 6.4 add_convert_fusion.2
  947.2 20.2 %fusion.39 = f32[2048,2048]{1,0:T(8,128)} fusion(bf16[2,1024,2048]{2,1,0:T(8,128)(2,1)} %param.33, f32[2048]{0:T(1024)S(1)} %bitcast.311, f32[2048,1024]{0,1:T(8,128)} %fusion.43, f32[2048,1024]{0,1:T(8,128)} %fusion.47), kind=kOutput, calls=%fused_computation.76 | convolution fusion | flops 8604614656 | bytes 37756928 | tf_op jit(solution)/shard_map/dot_general | solution.py:193
  967.4 21.8 %add_convert_fusion.1 = bf16[2048,2048]{1,0:T(8,128)(2,1)} fusion(f32[2048,2048]{1,0:T(8,128)} %fusion.39, bf16[2,1024,2048]{2,1,0:T(8,128)(2,1)} %param.33, f32[2048]{0:T(1024)S(1)} %bitcast.308, f32[2048,1024]{0,1:T(8,128)} %fusion.31, f32[2048,1024]{0,1:T(8,128)} %fusion.35), kind=kOutput, calls=%fused_computation.40 | convolution fusion | flops 8613003264 | bytes 46145536 | tf_op jit(solution)/shard_map/dot_general | solution.py:193
  994.0 4.2 maximum_convert_fusion
  998.2 5.3 copy.112
  1003.5 3.8 maximum_convert_fusion.1
  1007.3 5.3 copy.113
  1012.7 7.5 reduce-scatter.41.cloned.1.call-done
  1020.2 47.3 %reduce-scatter.39.cloned.1.call-done = bf16[256,2048]{1,0:T(8,128)(2,1)} async-done(((bf16[1024,2048]{1,0:T(8,128)(2,1)}), bf16[256,2048]{1,0:T(8,128)(2,1)}) %reduce-scatter.39.cloned.1.call-update) | async-done | bytes 1048592 | tf_op jit(solution)/shard_map/reduce_scatter | solution.py:240
  1067.5 3.8 maximum_convert_fusion.2
  1071.4 67.8 %reduce-scatter.29.cloned.1.call-done = bf16[512,256]{1,0:T(8,128)(2,1)} async-done(((bf16[512,2048]{1,0:T(8,128)(2,1)}), bf16[512,256]{1,0:T(8,128)(2,1)}) %reduce-scatter.29.cloned.1.call-update) | async-done | bytes 262160 | tf_op jit(solution)/shard_map/reduce_scatter | solution.py:358
  1141.0 68.5 %reduce-scatter.27.cloned.1.call-done = bf16[256,512]{1,0:T(8,128)(2,1)} async-done(((bf16[2048,512]{1,0:T(8,128)(2,1)}), bf16[256,512]{1,0:T(8,128)(2,1)}) %reduce-scatter.27.cloned.1.call-update) | async-done | bytes 262160 | tf_op jit(solution)/shard_map/reduce_scatter | solution.py:355
  1211.3 68.4 %reduce-scatter.23.cloned.1.call-done = bf16[256,512]{1,0:T(8,128)(2,1)} async-done(((bf16[2048,512]{1,0:T(8,128)(2,1)}), bf16[256,512]{1,0:T(8,128)(2,1)}) %reduce-scatter.23.cloned.1.call-update) | async-done | bytes 262160 | tf_op jit(solution)/shard_map/reduce_scatter | solution.py:349
  1281.5 69.1 %reduce-scatter.25.cloned.1.call-done = bf16[256,512]{1,0:T(8,128)(2,1)} async-done(((bf16[2048,512]{1,0:T(8,128)(2,1)}), bf16[256,512]{1,0:T(8,128)(2,1)}) %reduce-scatter.25.cloned.1.call-update) | async-done | bytes 262160 | tf_op jit(solution)/shard_map/reduce_scatter | solution.py:352
  1352.4 44.2 %reduce-scatter.21.cloned.1.call-done = bf16[256,2048]{1,0:T(8,128)(2,1)} async-done(((bf16[1024,2048]{1,0:T(8,128)(2,1)}), bf16[256,2048]{1,0:T(8,128)(2,1)}) %reduce-scatter.21.cloned.1.call-update) | async-done | bytes 1048592 | tf_op jit(solution)/shard_map/reduce_scatter | solution.py:335
  1398.5 151.1 %reduce-scatter.17.cloned.1.call-done = bf16[256,2048]{1,0:T(8,128)(2,1)} async-done(((bf16[2048,2048]{1,0:T(8,128)(2,1)}), bf16[256,2048]{1,0:T(8,128)(2,1)}) %reduce-scatter.17.cloned.1.call-update) | async-done | bytes 1048592 | tf_op jit(solution)/shard_map/reduce_scatter | solution.py:235
  1549.6 6.3 fusion.68
  1555.9 39.5 %all-reduce = (f32[2048]{0:T(1024)}, f32[128]{0:T(128)}, f32[128]{0:T(128)}, f32[2048]{0:T(1024)}) all-reduce(f32[2048]{0:T(1024)S(1)} %get-tuple-element.249, f32[128]{0:T(128)S(1)} %bitcast_reduce_fusion.1, f32[128]{0:T(128)S(1)} %bitcast_reduce_fusion, ...), channel_id=1, replica_groups=mesh['expert'=8,'tensor'=4] {'expert','tensor'}, use_global_device_ids=true, to_apply=%region_29.30 | all-reduce | flops 4352 | bytes 34816 | tf_op jit(solution)/shard_map/psum | solution.py:362
  (301 shorter events, 148.6 us)
Async XLA Ops:
  8.0 50.8 %copy-start = (bf16[2048,512]{1,0:T(8,128)(2,1)S(1)}, bf16[2048,512]{1,0:T(8,128)(2,1)}, u32[]{:S(2)}) copy-start(bf16[2048,512]{1,0:T(8,128)(2,1)} %param.23) | copy-start | bytes 6291460
  8.0 42.1 %all-gather.4.cloned.1.call-start = ((), (), s32[]{:S(2)}) async-start(), calls=%async_computation.15 | async-start | bytes 5242880 | tf_op jit(solution)/shard_map/all_gather | solution.py:121
  12.8 139.1 %reduce-scatter.15.cloned.1.call-start = ((), (), s32[]{:S(2)}) async-start(), calls=%async_computation.16 | async-start | bytes 5242880 | tf_op jit(solution)/shard_map/reduce_scatter | solution.py:156
  14.8 65.8 %copy-start.19 = (f32[1024,64]{1,0:T(8,128)}, f32[1024,64]{1,0:T(8,128)S(1)}, u32[]{:S(2)}) copy-start(f32[1024,64]{1,0:T(8,128)S(1)} %get-tuple-element.323) | copy-start | bytes 786436
  14.8 65.8 %copy-start.21 = (f32[1024,64]{1,0:T(8,128)}, f32[1024,64]{1,0:T(8,128)S(1)}, u32[]{:S(2)}) copy-start(f32[1024,64]{1,0:T(8,128)S(1)} %get-tuple-element.324) | copy-start | bytes 786436
  64.7 12.4 copy-start.32
  74.1 6.5 copy-start.30
  100.5 6.7 copy-start.3
  100.5 6.7 copy-start.34
  107.2 46.4 %copy-start.37 = (f32[2048]{0:T(1024)S(1)}, f32[2048]{0:T(1024)}, u32[]{:S(2)}) copy-start(f32[2048]{0:T(1024)} %param.29) | copy-start | bytes 24580
  107.2 44.7 %copy-start.8 = (bf16[256,2048]{1,0:T(8,128)(2,1)S(1)}, bf16[256,2048]{1,0:T(8,128)(2,1)}, u32[]{:S(2)}) copy-start(bf16[256,2048]{1,0:T(8,128)(2,1)} %param.19) | copy-start | bytes 3145732
  107.2 315.0 %all-gather.6.cloned.1.call-start = ((), (), s32[]{:S(2)}) async-start(), calls=%async_computation.18 | async-start | bytes 9437184 | tf_op jit(solution)/shard_map/all_gather | solution.py:117
  153.6 592.9 %copy-start.46 = (f32[256]{0:T(256)}, f32[256]{0:T(256)S(1)}, u32[]{:S(2)}) copy-start(f32[256]{0:T(256)S(1)} %add_rsqrt_fusion.2) | copy-start | bytes 3076
  156.2 27.8 %collective-permute-start = (bf16[256,2048]{1,0:T(8,128)(2,1)}, bf16[256,2048]{1,0:T(8,128)(2,1)S(1)}, u32[]{:S(2)}, u32[]{:S(2)}) collective-permute-start(bf16[256,2048]{1,0:T(8,128)(2,1)} %fusion.83), channel_id=1, source_target_pairs={{0,4},{4,8},{8,12},{12,16},{16,20},{20,24},{24,28},{28,0},{1,5},{5... | collective-permute-start | bytes 3145736 | tf_op jit(solution)/shard_map/ppermute | solution.py:26
  185.0 44.3 %collective-permute-start.1 = (bf16[256,2048]{1,0:T(8,128)(2,1)S(1)}, bf16[256,2048]{1,0:T(8,128)(2,1)}, u32[]{:S(2)}, u32[]{:S(2)}) collective-permute-start(bf16[256,2048]{1,0:T(8,128)(2,1)S(1)} %collective-permute-done), channel_id=1, source_target_pairs={{0,4},{4,8},{8,12},{12,16},{16,20},{20,24},{24,28},{28,0},{1,5},{5... | collective-permute-start | bytes 3145736 | tf_op jit(solution)/shard_map/ppermute | solution.py:26
  185.0 46.9 %collective-permute-start.4 = (bf16[256,2048]{1,0:T(8,128)(2,1)}, bf16[256,2048]{1,0:T(8,128)(2,1)}, u32[]{:S(2)}, u32[]{:S(2)}) collective-permute-start(bf16[256,2048]{1,0:T(8,128)(2,1)} %fusion.83), channel_id=1, source_target_pairs={{4,0},{8,4},{12,8},{16,12},{20,16},{24,20},{28,24},{0,28},{5,1},{9... | collective-permute-start | bytes 3145736 | tf_op jit(solution)/shard_map/ppermute | solution.py:28
  229.3 57.5 %collective-permute-start.2 = (bf16[256,2048]{1,0:T(8,128)(2,1)}, bf16[256,2048]{1,0:T(8,128)(2,1)}, u32[]{:S(2)}, u32[]{:S(2)}) collective-permute-start(bf16[256,2048]{1,0:T(8,128)(2,1)} %collective-permute-done.1), channel_id=1, source_target_pairs={{0,4},{4,8},{8,12},{12,16},{16,20},{20,24},{24,28},{28,0},{1,5},{5... | collective-permute-start | bytes 3145736 | tf_op jit(solution)/shard_map/ppermute | solution.py:26
  231.9 57.4 %collective-permute-start.5 = (bf16[256,2048]{1,0:T(8,128)(2,1)}, bf16[256,2048]{1,0:T(8,128)(2,1)}, u32[]{:S(2)}, u32[]{:S(2)}) collective-permute-start(bf16[256,2048]{1,0:T(8,128)(2,1)} %collective-permute-done.4), channel_id=1, source_target_pairs={{4,0},{8,4},{12,8},{16,12},{20,16},{24,20},{28,24},{0,28},{5,1},{9... | collective-permute-start | bytes 3145736 | tf_op jit(solution)/shard_map/ppermute | solution.py:28
  286.8 55.8 %collective-permute-start.3 = (bf16[256,2048]{1,0:T(8,128)(2,1)}, bf16[256,2048]{1,0:T(8,128)(2,1)}, u32[]{:S(2)}, u32[]{:S(2)}) collective-permute-start(bf16[256,2048]{1,0:T(8,128)(2,1)} %collective-permute-done.2), channel_id=1, source_target_pairs={{0,4},{4,8},{8,12},{12,16},{16,20},{20,24},{24,28},{28,0},{1,5},{5... | collective-permute-start | bytes 3145736 | tf_op jit(solution)/shard_map/ppermute | solution.py:26
  289.3 60.3 %copy-start.27 = (bf16[256,2048]{1,0:T(8,128)(2,1)S(1)}, bf16[256,2048]{1,0:T(8,128)(2,1)}, u32[]{:S(2)}) copy-start(bf16[256,2048]{1,0:T(8,128)(2,1)} %copy-done.26) | copy-start | bytes 3145732
  289.3 68.2 %collective-permute-start.6 = (bf16[256,2048]{1,0:T(8,128)(2,1)}, bf16[256,2048]{1,0:T(8,128)(2,1)S(1)}, u32[]{:S(2)}, u32[]{:S(2)}) collective-permute-start(bf16[256,2048]{1,0:T(8,128)(2,1)} %collective-permute-done.5), channel_id=1, source_target_pairs={{4,0},{8,4},{12,8},{16,12},{20,16},{24,20},{28,24},{0,28},{5,1},{9... | collective-permute-start | bytes 3145736 | tf_op jit(solution)/shard_map/ppermute | solution.py:28
  367.2 14.8 copy-start.18
  442.0 23.8 %copy-start.62 = (f32[2048,16]{0,1:T(8,128)S(1)}, f32[2048,16]{0,1:T(8,128)}, u32[]{:S(2)}) copy-start(f32[2048,16]{0,1:T(8,128)} %param.30) | copy-start | bytes 393220
  442.0 30.3 %copy-start.43 = (s32[256,8]{0,1:T(8,128)S(1)}, s32[256,8]{0,1:T(8,128)}, u32[]{:S(2)}) copy-start(s32[256,8]{0,1:T(8,128)} %param.21) | copy-start | bytes 24580
  462.2 10.1 all-to-all-start
  465.7 275.8 %reduce-scatter.19.cloned.1.call-start = ((), (), s32[]{:S(2)}) async-start(), calls=%async_computation.19 | async-start | bytes 9437184 | tf_op jit(solution)/shard_map/reduce_scatter | solution.py:221
  472.5 269.0 %copy-start.48 = (f32[256,16]{0,1:T(8,128)}, f32[256,16]{0,1:T(8,128)S(1)}, u32[]{:S(2)}) copy-start(f32[256,16]{0,1:T(8,128)S(1)} %get-tuple-element.251) | copy-start | bytes 49156
  503.1 304.0 %copy-start.39 = (f32[2048,1]{0,1:T(1,128)}, f32[2048,1]{0,1:T(1,128)S(1)}, u32[]{:S(2)}) copy-start(f32[2048,1]{0,1:T(1,128)S(1)} %get-tuple-element.321) | copy-start | bytes 24580
  503.1 320.9 %copy-start.41 = (f32[2048,1]{0,1:T(1,128)}, f32[2048,1]{0,1:T(1,128)S(1)}, u32[]{:S(2)}) copy-start(f32[2048,1]{0,1:T(1,128)S(1)} %get-tuple-element.322) | copy-start | bytes 24580
  515.6 15.8 copy-start.24
  515.6 15.8 slice-start
  515.6 15.8 slice-start.1
  540.6 16.9 %copy-start.23 = (bf16[2048,1024]{0,1:T(8,128)(2,1)}, bf16[2048,1024]{0,1:T(8,128)(2,1)S(1)}, u32[]{:S(2)}) copy-start(bf16[2048,1024]{0,1:T(8,128)(2,1)S(1)} %get-tuple-element.301) | copy-start | bytes 12582916
  597.2 243.4 %all-gather.8.cloned.1.call-start = ((), (), s32[]{:S(2)}) async-start(), calls=%async_computation.20 | async-start | bytes 5242880 | tf_op jit(solution)/shard_map/all_gather | solution.py:263
  741.5 6.3 copy-start.13
  741.5 6.3 copy-start.14
  746.4 17.4 %copy-start.50 = (f32[256]{0:T(256)}, f32[256]{0:T(256)S(1)}, u32[]{:S(2)}) copy-start(f32[256]{0:T(256)S(1)} %broadcast_multiply_fusion.3) | copy-start | bytes 3076
  749.9 244.0 %reduce-scatter.33.cloned.1.call-start = ((), (), s32[]{:S(2)}) async-start(), calls=%async_computation.28 | async-start | bytes 5242880 | tf_op jit(solution)/shard_map/reduce_scatter | solution.py:240
  763.8 230.2 %reduce-scatter.31.cloned.1.call-start = ((), (), s32[]{:S(2)}) async-start(), calls=%async_computation.27 | async-start | bytes 5242880 | tf_op jit(solution)/shard_map/reduce_scatter | solution.py:240
  778.0 225.5 %reduce-scatter.37.cloned.1.call-start = ((), (), s32[]{:S(2)}) async-start(), calls=%async_computation.30 | async-start | bytes 5242880 | tf_op jit(solution)/shard_map/reduce_scatter | solution.py:240
  791.9 211.6 %reduce-scatter.35.cloned.1.call-start = ((), (), s32[]{:S(2)}) async-start(), calls=%async_computation.29 | async-start | bytes 5242880 | tf_op jit(solution)/shard_map/reduce_scatter | solution.py:240
  807.0 213.2 %reduce-scatter.41.cloned.1.call-start = ((), (), s32[]{:S(2)}) async-start(), calls=%async_computation.32 | async-start | bytes 5242880 | tf_op jit(solution)/shard_map/reduce_scatter | solution.py:240
  823.9 243.6 %reduce-scatter.39.cloned.1.call-start = ((), (), s32[]{:S(2)}) async-start(), calls=%async_computation.31 | async-start | bytes 5242880 | tf_op jit(solution)/shard_map/reduce_scatter | solution.py:240
  840.5 298.7 %reduce-scatter.29.cloned.1.call-start = ((), (), s32[]{:S(2)}) async-start(), calls=%async_computation.25 | async-start | bytes 2359296 | tf_op jit(solution)/shard_map/reduce_scatter | solution.py:358
  848.1 6.4 copy-start.4
  848.1 6.4 copy-start.35
  854.4 355.1 %reduce-scatter.27.cloned.1.call-start = ((), (), s32[]{:S(2)}) async-start(), calls=%async_computation.24 | async-start | bytes 2359296 | tf_op jit(solution)/shard_map/reduce_scatter | solution.py:355
  887.9 7.0 copy-start.54
  894.9 3.2 copy-start.20
  894.9 3.2 copy-start.22
  894.9 384.8 %reduce-scatter.23.cloned.1.call-start = ((), (), s32[]{:S(2)}) async-start(), calls=%async_computation.22 | async-start | bytes 2359296 | tf_op jit(solution)/shard_map/reduce_scatter | solution.py:349
  898.1 7.5 copy-start.12
  911.0 3.4 copy-start.57
  914.5 3.9 copy-start.56
  918.4 432.3 %reduce-scatter.25.cloned.1.call-start = ((), (), s32[]{:S(2)}) async-start(), calls=%async_computation.23 | async-start | bytes 2359296 | tf_op jit(solution)/shard_map/reduce_scatter | solution.py:352
  926.6 4.2 copy-start.58
  934.7 461.9 %reduce-scatter.21.cloned.1.call-start = ((), (), s32[]{:S(2)}) async-start(), calls=%async_computation.21 | async-start | bytes 5242880 | tf_op jit(solution)/shard_map/reduce_scatter | solution.py:335
  946.5 20.9 %copy-start.40 = (f32[2048,1]{0,1:T(1,128)S(1)}, f32[2048,1]{0,1:T(1,128)}, u32[]{:S(2)}) copy-start(f32[2048,1]{0,1:T(1,128)} %copy-done.39) | copy-start | bytes 24580
  946.5 603.1 %reduce-scatter.17.cloned.1.call-start = ((), (), s32[]{:S(2)}) async-start(), calls=%async_computation.17 | async-start | bytes 9437184 | tf_op jit(solution)/shard_map/reduce_scatter | solution.py:235
  989.3 606.1 %all-reduce.3.cloned.1.call-start = ((), (), s32[]{:S(2)}) async-start(), calls=%async_computation.26 | async-start | bytes 262144 | tf_op jit(solution)/shard_map/psum | solution.py:362
  1067.5 329.1 %copy-start.36 = (f32[2048]{0:T(1024)S(1)}, f32[2048]{0:T(1024)}, u32[]{:S(2)}) copy-start(f32[2048]{0:T(1024)} %param.22) | copy-start | bytes 24580
  1067.5 329.1 %copy-start.45 = (f32[256]{0:T(256)S(1)}, f32[256]{0:T(256)}, u32[]{:S(2)}) copy-start(f32[256]{0:T(256)} %copy-done.44) | copy-start | bytes 3076
  1071.4 478.2 %copy-start.51 = (f32[256]{0:T(256)S(1)}, f32[256]{0:T(256)}, u32[]{:S(2)}) copy-start(f32[256]{0:T(256)} %copy-done.50) | copy-start | bytes 3076
  1398.5 157.4 %copy-start.52 = (f32[2048]{0:T(1024)S(1)}, f32[2048]{0:T(1024)}, u32[]{:S(2)}) copy-start(f32[2048]{0:T(1024)} %get-tuple-element.247) | copy-start | bytes 24580
  (38 other events, 69.5 us)
Sparse Core Ops, SparseCore 0:
  12.9 37.1 all-gather.3
  107.4 44.5 reduce-scatter.14
  750.0 33.5 all-gather.7
  786.1 44.5 reduce-scatter.32
  833.7 44.5 reduce-scatter.30
  881.2 44.5 reduce-scatter.36
  928.5 44.5 reduce-scatter.34
  975.6 44.5 reduce-scatter.40
  1022.9 44.5 reduce-scatter.38
  1070.9 68.2 reduce-scatter.28
  1142.8 66.7 reduce-scatter.26
  1212.9 66.7 reduce-scatter.22
  1283.8 66.7 reduce-scatter.24
  1353.0 43.5 reduce-scatter.20
  1400.5 148.9 reduce-scatter.16
Sparse Core Ops, SparseCore 1:
  231.9 174.2 all-gather.5
  597.3 144.2 reduce-scatter.18
  995.9 159.5 all-reduce.2
